TPU v7x, 32 devices: a whole 2x2x4 slice. The times are simulated.
32 devices in a mesh: replica: 2 (over y), section: 2 (over core), seq: 8 (over z, x).
Axes of the slice: x: 2, y: 2, z: 4, core: 2. Of those that a mesh axis runs over, the one named last changes fastest.
Arguments:
- latents: float32 [2, 1024, 64], P('section', ('replica', 'seq')), parts along dimension 1, may hold values from -6 to 6
- cond: bfloat16 [2, 3, 1024, 4096], P('section', None, ('replica', 'seq')), parts along dimension 2, may hold values from -60 to 60
- embed: bfloat16 [2, 3, 64, 4096], P('section'), may hold values from -0.75 to 0.75
- audio_table: bfloat16 [2, 64, 4096], P('section', 'replica'), parts along dimension 1, may hold values from -6 to 6
- audio_map: int32 [64], P(('replica', 'seq')), parts along dimension 0, may hold values from 0 to 31
- out_proj: bfloat16 [2, 4096, 64], P('section'), may hold values from -0.5 to 0.5
- tile_start: int32 [16], P('replica'), parts along dimension 0, may hold values 0 or 1
- conv_input: bfloat16 [3, 3, 16, 512], P(None, None, None, 'section'), may hold values from -0.5 to 0.5
- conv_first: bfloat16 [3, 3, 512, 512], P(None, None, None, 'section'), may hold values from -0.09375 to 0.09375
- conv_second_up: bfloat16 [3, 3, 512, 256], P(None, None, None, 'section'), may hold values from -0.09375 to 0.09375
- conv_second: bfloat16 [3, 3, 256, 256], P(None, None, None, 'section'), may hold values from -0.125 to 0.125
- conv_third_up: bfloat16 [3, 3, 256, 128], P(None, None, None, 'section'), may hold values from -0.125 to 0.125
- conv_third: bfloat16 [3, 3, 128, 128], P(None, None, None, 'section'), may hold values from -0.1875 to 0.1875
- conv_color: bfloat16 [3, 3, 128, 3], replicated, may hold values from -0.1875 to 0.1875
- gain_first: float32 [512], replicated, may hold values from 0.1 to 1.9
- gain_second: float32 [256], replicated, may hold values from 0.1 to 1.9
- gain_third: float32 [128], replicated, may hold values from 0.1 to 1.9
- gain_color: float32 [128], replicated, may hold values from 0.1 to 1.9
Outputs:
- handoff: float32 [2, 1024, 64], P('section', ('replica', 'seq')), parts along dimension 1
- image: float32 [3, 128, 512], P(None, ('replica', 'seq')), parts along dimension 1
There are 2 independent parts, one for each index of `replica`. A program takes and returns all parts, laid end to end along the dimension named above; an argument that names none is the same for every part. Nothing has to cross between parts.
Inputs may be any that keep to these rules, and one draw needn't show every extreme that they name: `tile_start`: entry i is 1 where a decoder row tile begins at row block i; entry 0 is not read.
All inputs are finite; a program needn't handle non-finite values.
Results may differ from a plain program's by a relative error of at most 0.017.
Values may be sent and summed in bfloat16 or wider, within the bound.
A program may use at most 128 MiB of HBM per device.

v0:
```python
import functools
import math

import jax
import jax.numpy as jnp
from jax import lax
from jax.experimental import pallas as pl
from jax.experimental.pallas import tpu as pltpu
from jax.sharding import PartitionSpec as P

HEADS = 32
HSIZE = 128


step_size = -0.5
norm_eps = 1e-06


MESH = pl.DeviceIdType.MESH


def lift(weight, lifted):
    depth = weight.shape[1]
    chunk = 64

    @pl.loop(0, depth // chunk)
    def _(i):
        row = pl.multiple_of(i * chunk, chunk)
        w = [weight[t, pl.ds(row, chunk)].astype(jnp.float32) for t in range(9)]

        def pairs(x, y, z):
            return ((x, y + z), (x + y, z))

        by_row = [pairs(w[q], w[3 + q], w[6 + q]) for q in range(3)]
        for a in (0, 1):
            for p in (0, 1):
                cols = pairs(*(by_row[q][a][p] for q in range(3)))
                for b in (0, 1):
                    for q in (0, 1):
                        at = pl.multiple_of((2 * p + q) * depth + row, chunk)
                        lifted[2 * a + b, pl.ds(at, chunk)] = cols[b][q].astype(jnp.bfloat16)


def front_kernel(
    splits, heads_here, sections, devices,
    latent, cond, embed, table, picks, out_proj, up2, up3, w_in, w_first, w_second, w_third,
    handed, tokens, o_up2, o_up3, i_up2, i_up3, i_in, i_first, i_second, i_third,
    proj, got_q, got_kv, partial, parts, result, low_final, rows, got_result, l_up2, l_up3,
    send_q, recv_q, send_kv, recv_kv, own_sem, send_p, recv_p, send_w, recv_w, keep_sem,
    send_h, recv_h, send_r, recv_r,
):
    f32, bf16 = jnp.float32, jnp.bfloat16
    me = lax.axis_index("seq")
    section = lax.axis_index("section")
    groups = devices // splits
    count = latent.shape[0]
    half = count // splits
    width = got_q.shape[1]
    size = width // heads_here
    my_group = me // splits

    barrier = pltpu.get_barrier_semaphore()
    for t in range(sections):

        @pl.loop(0, devices)
        def _(d):
            @pl.when(jnp.logical_or(d != me, section != t))
            def _():
                pl.semaphore_signal(
                    barrier, inc=1, device_id={"section": t, "seq": d}, device_id_type=MESH
                )

    pl.semaphore_wait(barrier, sections * devices - 1)

    low = latent[...].astype(bf16)
    partner = {"section": lax.rem(section + 1, sections)}

    def weight_copy(src, dst, k):
        return pltpu.make_async_remote_copy(
            src_ref=src, dst_ref=dst, send_sem=send_w.at[k], recv_sem=recv_w.at[k],
            device_id=partner, device_id_type=MESH,
        )

    def q_copy(d, src):
        return pltpu.make_async_remote_copy(
            src_ref=proj.at[d // splits, 0, pl.ds(lax.rem(d, splits) * half, half)],
            dst_ref=got_q.at[pl.ds(src * half, half)],
            send_sem=send_q.at[d], recv_sem=recv_q.at[src],
            device_id={"seq": d}, device_id_type=MESH,
        )

    def kv_copy(d, src):
        return pltpu.make_async_remote_copy(
            src_ref=proj.at[d // splits, pl.ds(1, 2)],
            dst_ref=got_kv.at[:, pl.ds(src * count, count)],
            send_sem=send_kv.at[d], recv_sem=recv_kv.at[src],
            device_id={"seq": d}, device_id_type=MESH,
        )

    @pl.loop(0, groups)
    def _(k):
        g = lax.rem(my_group + 1 + k, groups)
        lanes = pl.ds(pl.multiple_of(g * width, 128), width)
        audio = jnp.dot(picks[...], table[:, lanes], preferred_element_type=f32)
        for c in range(3):
            value = jnp.dot(low, embed[c, :, lanes], preferred_element_type=f32)
            value = value + cond[c, :, lanes].astype(f32)
            if c != 1:
                value = value + audio
            proj[g, c] = value.astype(bf16)

        @pl.loop(0, splits)
        def _(r):
            d = g * splits + r

            @pl.when(d != me)
            def _():
                q_copy(d, me).start()
                kv_copy(d, me).start()

    own_q = pltpu.make_async_copy(
        proj.at[my_group, 0, pl.ds(lax.rem(me, splits) * half, half)],
        got_q.at[pl.ds(me * half, half)], own_sem.at[0],
    )
    own_kv = pltpu.make_async_copy(
        proj.at[my_group, pl.ds(1, 2)], got_kv.at[:, pl.ds(me * count, count)], own_sem.at[1]
    )
    own_q.start()
    own_kv.start()
    plain = [
        weight_copy(w_in, i_in, 0), weight_copy(w_first, i_first, 1),
        weight_copy(w_second, i_second, 2), weight_copy(w_third, i_third, 3),
    ]
    for copy in plain:
        copy.start()
    lift(up2, l_up2)
    lift(up3, l_up3)
    made = [weight_copy(l_up2, i_up2, 4), weight_copy(l_up3, i_up3, 5)]
    kept = [
        pltpu.make_async_copy(l_up2, o_up2, keep_sem.at[0]),
        pltpu.make_async_copy(l_up3, o_up3, keep_sem.at[1]),
    ]
    for copy in made + kept:
        copy.start()

    own_q.wait()
    own_kv.wait()

    @pl.loop(0, devices)
    def _(d):
        @pl.when(d != me)
        def _():
            q_copy(d, d).wait_recv()
            kv_copy(d, d).wait_recv()

    query_count = got_q.shape[0]
    block = min(256, query_count)
    scale = 1.0 / math.sqrt(size)

    @pl.loop(0, query_count // block)
    def _(i):
        at = pl.ds(pl.multiple_of(i * block, block), block)
        total = jnp.zeros((block, out_proj.shape[1]), f32)
        for h in range(heads_here):
            lanes = slice(h * size, (h + 1) * size)
            scores = lax.dot_general(
                got_q[at, lanes], got_kv[0, :, lanes], (((1,), (1,)), ((), ())),
                preferred_element_type=f32,
            ) * scale
            row_max = jnp.max(scores, axis=1, keepdims=True)
            weights = jnp.exp(scores - row_max)
            denominator = jnp.sum(weights, axis=1, keepdims=True)
            attended = jnp.dot(
                weights.astype(bf16), got_kv[1, :, lanes], preferred_element_type=f32
            ) / denominator
            rows_of = pl.ds(pl.multiple_of(my_group * width + h * size, size), size)
            total = total + jnp.dot(
                attended.astype(bf16), out_proj[rows_of], preferred_element_type=f32
            )
        partial[at] = total

    def part_copy(d, src):
        return pltpu.make_async_remote_copy(
            src_ref=partial.at[pl.ds(d * half, half)],
            dst_ref=parts.at[src],
            send_sem=send_p.at[d], recv_sem=recv_p.at[src],
            device_id={"seq": d}, device_id_type=MESH,
        )

    @pl.loop(0, devices)
    def _(k):
        d = lax.rem(me + k, devices)

        @pl.when(d != me)
        def _():
            part_copy(d, me).start()

    @pl.loop(0, devices)
    def _(d):
        @pl.when(d != me)
        def _():
            part_copy(d, d).wait_recv()

    for r in range(splits):
        at = slice(r * half, (r + 1) * half)

        def add(g, total):
            d = g * splits + r
            own = partial[pl.ds(pl.multiple_of(me * half, half), half)]
            return total + jnp.where(d == me, own, parts[d])

        velocity = lax.fori_loop(0, groups, add, jnp.zeros((half, latent.shape[1]), f32))
        result[at] = latent[at] + step_size * velocity
    low_final[...] = result[...].astype(bf16)

    last = section == sections - 1
    given = pltpu.make_async_remote_copy(
        src_ref=result, dst_ref=got_result, send_sem=send_r, recv_sem=recv_r,
        device_id=partner, device_id_type=MESH,
    )
    given.start()

    def row_copy(by, t, to):
        slot = {2: 0, 1: 1, -1: 2, -2: 3}[by]
        return pltpu.make_async_remote_copy(
            src_ref=low_final, dst_ref=rows.at[slot],
            send_sem=send_h.at[slot, t], recv_sem=recv_h.at[slot],
            device_id={"section": t, "seq": lax.rem(to + devices, devices)}, device_id_type=MESH,
        )

    for by in (2, -2, 1, -1):
        for t in range(sections):
            inside = jnp.logical_and(me + by >= 0, me + by < devices)

            @pl.when(jnp.logical_and(last, inside))
            def _():
                row_copy(by, t, me + by).start()

    given.wait_recv()
    handed[...] = got_result[...]

    @pl.when(last)
    def _():
        tokens[2] = low_final[...]

    @pl.when(jnp.logical_not(last))
    def _():
        tokens[2] = got_result[...].astype(bf16)

    for by, slot, at in ((2, 0, 0), (1, 1, 1), (-1, 2, 3), (-2, 3, 4)):
        inside = jnp.logical_and(me - by >= 0, me - by < devices)

        @pl.when(inside)
        def _():
            row_copy(by, 0, me - by).wait_recv()
            tokens[at] = rows[slot]

        @pl.when(jnp.logical_not(inside))
        def _():
            tokens[at] = jnp.zeros(tokens.shape[1:], bf16)

    for by in (2, -2, 1, -1):
        for t in range(sections):
            inside = jnp.logical_and(me + by >= 0, me + by < devices)

            @pl.when(jnp.logical_and(last, inside))
            def _():
                row_copy(by, t, me + by).wait_send()

    given.wait_send()

    @pl.loop(0, devices)
    def _(d):
        @pl.when(d != me)
        def _():
            q_copy(d, me).wait_send()
            kv_copy(d, me).wait_send()
            part_copy(d, me).wait_send()

    for copy in kept + plain + made:
        copy.wait()


def front(latent, cond, embed, table, picks, out_proj, halves, splits, groups, width):
    w_in, w_first, up2, w_second, up3, w_third = halves
    devices, sections = lax.axis_size("seq"), lax.axis_size("section")
    f32, bf16 = jnp.float32, jnp.bfloat16
    count, patch = latent.shape
    half = count // splits
    heads_here = width // HSIZE
    vmem, hbm = pl.BlockSpec(memory_space=pltpu.VMEM), pl.BlockSpec(memory_space=pl.ANY)
    like = lambda a: jax.ShapeDtypeStruct(a.shape, a.dtype)
    lifted = lambda w: jax.ShapeDtypeStruct((4, 4 * w.shape[1], w.shape[2]), bf16)
    dma = pltpu.SemaphoreType.DMA
    l2, l3 = lifted(up2), lifted(up3)
    return pl.pallas_call(
        functools.partial(front_kernel, splits, heads_here, sections, devices),
        out_shape=(
            like(latent), jax.ShapeDtypeStruct((5, count, patch), bf16),
            l2, l3, l2, l3, like(w_in), like(w_first), like(w_second), like(w_third),
        ),
        in_specs=[vmem] * 8 + [hbm] * 4,
        out_specs=(vmem, vmem) + (hbm,) * 8,
        scratch_shapes=[
            pltpu.VMEM((groups, 3, count, width), bf16),
            pltpu.VMEM((devices * half, width), bf16),
            pltpu.VMEM((2, devices * count, width), bf16),
            pltpu.VMEM((devices * half, patch), f32),
            pltpu.VMEM((devices, half, patch), f32),
            pltpu.VMEM((count, patch), f32),
            pltpu.VMEM((count, patch), bf16),
            pltpu.VMEM((4, count, patch), bf16),
            pltpu.VMEM((count, patch), f32),
            pltpu.VMEM(l2.shape, bf16),
            pltpu.VMEM(l3.shape, bf16),
            dma((devices,)), dma((devices,)), dma((devices,)), dma((devices,)), dma((2,)),
            dma((devices,)), dma((devices,)), dma((6,)), dma((6,)), dma((2,)),
            dma((4, sections)), dma((4,)), dma, dma,
        ],
        compiler_params=pltpu.CompilerParams(
            collective_id=0, has_side_effects=True, vmem_limit_bytes=48 * 1024 * 1024
        ),
    )(latent, cond, embed, table, picks, out_proj, up2, up3, w_in, w_first, w_second, w_third)


def decode_kernel(
    keep, tokens, w_color, g1, g2, g3, g4,
    h_in, h_first, h_up2, h_second, h_up3, h_third,
    t_in, t_first, t_up2, t_second, t_up3, t_third,
    out, a1, p1, x1, a2, p2, x2, a3, p3, p4,
    w_in, w_first, w_up2, w_second, b_up3, b_third, w_up3, w_third, sems,
):
    section = lax.axis_index("section")
    loads = []
    for own, source in ((0, (h_in, h_first, h_up2, h_second, h_up3, h_third)),
                        (1, (t_in, t_first, t_up2, t_second, t_up3, t_third))):
        place = lax.rem(section + own, 2)
        for k, (src, dst) in enumerate(
            zip(source, (w_in, w_first, w_up2, w_second, b_up3, b_third))
        ):
            if k < 4:
                lanes = src.shape[-1]
                at = pl.ds(pl.multiple_of(place * lanes, 128), lanes)
                view = dst.at[:, :, at] if len(dst.shape) == 3 else dst.at[:, at]
            else:
                view = dst.at[place]
            copy = pltpu.make_async_copy(src, view, sems.at[own, k])
            copy.start()
            loads.append((k, copy))

    def ready(index):
        for k, copy in loads:
            if k == index:
                copy.wait()

    cols = tokens.shape[1]
    f32, bf16 = jnp.float32, jnp.bfloat16
    k_a, k_b, k_c, k_d = keep[0], keep[1], keep[2], keep[3]

    def moved(value, by):
        position = lax.broadcasted_iota(jnp.int32, value.shape, 0)
        if by > 0:
            return jnp.where(position > 0, pltpu.roll(value, 1, 0), 0.0)
        return jnp.where(position < cols - 1, pltpu.roll(value, cols - 1, 0), 0.0)

    def put(buf, index, value):
        phases = value.shape[0]
        buf[index, 1 : phases + 1] = value.astype(bf16)
        buf[index, 0] = moved(value[phases - 1], 1).astype(bf16)
        buf[index, phases + 1] = moved(value[0], -1).astype(bf16)

    def act(value, gain):
        square = jnp.mean(value * value, axis=-1, keepdims=True)
        scaled = value * lax.rsqrt(square + norm_eps) * gain[...]
        return jax.nn.silu(scaled)

    def fill(source, buf, count, where_to, masked, gain=None, offset=0):
        @pl.loop(0, count)
        def _(i):
            value = source[i + offset].astype(f32)
            put(buf, where_to(i), value if gain is None else act(value, gain))

        for target, origin, factor in masked:
            if origin is None:
                buf[target] = jnp.zeros(buf.shape[1:], bf16)
            else:
                buf[target] = (buf[origin].astype(f32) * factor).astype(bf16)

    def spots(*bounds):
        def start(o):
            index = o
            for bound in bounds:
                index = index + 2 * (o >= bound).astype(jnp.int32)
            return index

        return start

    def window(buf, start, rows, taps_r, taps_c, phases):
        parts = []
        for p in taps_r:
            for q in taps_c:
                block = buf[pl.ds(start + p, rows), q : q + phases]
                parts.append(block.reshape(rows * phases * cols, block.shape[-1]))
        return jnp.concatenate(parts, axis=1)

    def dot(x, w):
        return jnp.dot(x, w, preferred_element_type=f32)

    full = tokens[...].astype(f32)
    count = full.shape[0]
    zero = jnp.zeros((1,) + full.shape[1:], f32)
    ks = (k_a, k_b, k_c, k_d)
    above = jnp.concatenate([zero] + [full[i : i + 1] * ks[i] for i in range(count - 1)])
    below = jnp.concatenate([full[i + 1 : i + 2] * ks[i] for i in range(count - 1)] + [zero])
    pieces = []
    for rows in (above, full, below):
        left = jnp.stack([moved(rows[i], 1) for i in range(count)])
        right = jnp.stack([moved(rows[i], -1) for i in range(count)])
        pieces += [left, rows, right]
    x = jnp.concatenate(pieces, axis=2).astype(bf16).reshape(count * cols, -1)
    cell = tokens.shape[2]
    chans = cell // 4
    column = lax.broadcasted_iota(jnp.int32, (9 * cell, 9 * chans), 1)
    line = lax.broadcasted_iota(jnp.int32, (9 * cell, 9 * chans), 0)
    tap = column // chans
    tap_r = (tap >= 3).astype(jnp.int32) + (tap >= 6).astype(jnp.int32)
    tap_c = tap - 3 * tap_r
    ready(0)
    for a in (0, 1):
        for b in (0, 1):
            u, v = tap_r + (a + 1), tap_c + (b + 1)
            wanted = ((u >> 1) * 3 + (v >> 1)) * cell + (2 * (u & 1) + (v & 1)) * chans
            pick = (line == wanted + column - tap * chans).astype(f32).astype(bf16)
            y = dot(dot(x, pick).astype(bf16), w_in[...]).astype(bf16)
            for i in range(count):
                a1[2 * i + a, b] = y[i * cols : (i + 1) * cols]

    def spot1(i):
        return i + 1 + 2 * (i >= 2).astype(jnp.int32) + 2 * (i >= 4).astype(jnp.int32)

    inner = ((3, 5, k_b), (4, 2, k_b), (7, 9, k_c), (8, 6, k_c))
    fill(a1, p1, 6, spot1, inner, g1, 2)
    for target, origin, factor in ((0, 1, k_a), (11, 8, k_d)):
        put(p1, target, act(a1[origin].astype(f32), g1) * factor)
    ready(1)

    @pl.loop(0, 3)
    def _(i):
        y = dot(window(p1, 4 * i, 2, (0, 1, 2), (0, 1, 2), 2), w_first[...])
        base = a1[pl.ds(2 * i + 2, 2)]
        a1[pl.ds(2 * i + 2, 2)] = (base.astype(f32) + y.reshape(base.shape)).astype(bf16)

    fill(a1, x1, 6, spot1, inner + ((0, None, 0), (11, None, 0)), None, 2)

    ready(2)
    @pl.loop(0, 3)
    def _(i):
        for a in (0, 1):
            for b in (0, 1):
                y = dot(window(x1, 4 * i, 2, (a, a + 1), (b, b + 1), 2), w_up2[2 * a + b])
                y = y.astype(bf16).reshape(2, 2, cols, -1)
                for r in (0, 1):
                    for f in (0, 1):
                        a2[4 * i + 2 * r + a, 2 * f + b] = y[r, f]

    fill(
        a2, p2, 10,
        lambda i: i + 2 * (i >= 3).astype(jnp.int32) + 2 * (i >= 7).astype(jnp.int32),
        ((3, 5, k_b), (4, 2, k_b), (9, 11, k_c), (10, 8, k_c)), g2, 1,
    )
    start2 = spots(2, 6)
    ready(3)

    @pl.loop(0, 8)
    def _(o):
        y = dot(window(p2, start2(o), 1, (0, 1, 2), (0, 1, 2), 4), w_second[...])
        base = a2[o + 2]
        a2[o + 2] = (base.astype(f32) + y.reshape(base.shape)).astype(bf16)

    fill(
        a2, x2, 8,
        lambda i: i + 2 * (i >= 2).astype(jnp.int32) + 2 * (i >= 6).astype(jnp.int32),
        ((2, 4, k_b), (3, 1, k_b), (8, 10, k_c), (9, 7, k_c)), None, 2,
    )
    start3 = spots(1, 5)

    ready(4)
    ready(5)
    w_up3[...] = jnp.concatenate([b_up3[0], b_up3[1]], axis=2)
    w_third[...] = jnp.concatenate([b_third[0], b_third[1]], axis=1)

    @pl.loop(0, 6)
    def _(o):
        for a in (0, 1):
            for b in (0, 1):
                y = dot(window(x2, start3(o), 1, (a, a + 1), (b, b + 1), 4), w_up3[2 * a + b])
                y = y.astype(bf16).reshape(4, cols, -1)
                for f in range(4):
                    a3[2 * o + a, 2 * f + b] = y[f]

    fill(
        a3, p3, 12,
        lambda i: i + 2 * (i >= 2).astype(jnp.int32) + 2 * (i >= 10).astype(jnp.int32),
        ((2, 4, k_b), (3, 1, k_b), (12, 14, k_c), (13, 11, k_c)), g3,
    )
    start4 = spots(1, 9)

    @pl.loop(0, 10)
    def _(o):
        y = dot(window(p3, start4(o), 1, (0, 1, 2), (0, 1, 2), 8), w_third[...])
        base = a3[o + 1]
        value = (base.astype(f32) + y.reshape(base.shape)).astype(bf16).astype(f32)
        put(p4, o, act(value, g4))

    for target, factor in ((0, k_b), (9, k_c)):
        p4[target] = (p4[target].astype(f32) * factor).astype(bf16)

    @pl.loop(0, 8)
    def _(o):
        patch = window(p4, o, 1, (0, 1, 2), (0, 1, 2), 8)
        colors = lax.dot_general(
            w_color[...], patch, (((1,), (1,)), ((), ())), preferred_element_type=f32
        )
        for k in range(out.shape[0]):
            out[k, pl.ds(o, 1)] = colors[k : k + 1]


def decode(tokens, keep, color, gains, own, other, rgb):
    count, cols = tokens.shape[:2]
    c1, c2, c3 = (2 * own[k].shape[-1] for k in (1, 3, 5))
    bf16 = jnp.bfloat16
    vmem, hbm = pl.BlockSpec(memory_space=pltpu.VMEM), pl.BlockSpec(memory_space=pl.ANY)
    wide = lambda w: pltpu.VMEM(w.shape[:-1] + (2 * w.shape[-1],), bf16)
    return pl.pallas_call(
        decode_kernel,
        out_shape=jax.ShapeDtypeStruct((rgb, 8, 8 * cols), jnp.float32),
        in_specs=[pl.BlockSpec(memory_space=pltpu.SMEM)] + [vmem] * 6 + [hbm] * 12,
        out_specs=vmem,
        scratch_shapes=[
            pltpu.VMEM((2 * count, 2, cols, c1), bf16),
            pltpu.VMEM((12, 4, cols, c1), bf16),
            pltpu.VMEM((12, 4, cols, c1), bf16),
            pltpu.VMEM((12, 4, cols, c2), bf16),
            pltpu.VMEM((14, 6, cols, c2), bf16),
            pltpu.VMEM((12, 6, cols, c2), bf16),
            pltpu.VMEM((12, 8, cols, c3), bf16),
            pltpu.VMEM((16, 10, cols, c3), bf16),
            pltpu.VMEM((10, 10, cols, c3), bf16),
            wide(own[0]), wide(own[1]), wide(own[2]), wide(own[3]),
            pltpu.VMEM((2,) + own[4].shape, bf16), pltpu.VMEM((2,) + own[5].shape, bf16),
            wide(own[4]), wide(own[5]),
            pltpu.SemaphoreType.DMA((2, 6)),
        ],
        compiler_params=pltpu.CompilerParams(vmem_limit_bytes=56 * 1024 * 1024),
    )(keep, tokens, color, *gains, *own, *other)


def body(
    latents,
    cond,
    embed,
    audio_table,
    audio_map,
    out_proj,
    tile_start,
    conv_input,
    conv_first,
    conv_second_up,
    conv_second,
    conv_third_up,
    conv_third,
    conv_color,
    gain_first,
    gain_second,
    gain_third,
    gain_color,
):
    latent = latents[0]
    tokens_here = latent.shape[0]
    frame_count = audio_table.shape[1]
    frames = jnp.repeat(audio_map, tokens_here // audio_map.shape[0])
    picks = (frames[:, None] == lax.broadcasted_iota(jnp.int32, (1, frame_count), 1)).astype(
        jnp.bfloat16
    )
    devices = lax.axis_size("seq")
    splits = max(devices // HEADS, 1)
    per_device = max(HEADS // devices, 1)
    groups = HEADS // per_device
    flat = lambda w: w.reshape(-1, w.shape[-1])
    taps = lambda w: w.reshape(9, *w.shape[2:])
    halves = (
        flat(conv_input), flat(conv_first), taps(conv_second_up),
        flat(conv_second), taps(conv_third_up), flat(conv_third),
    )
    handed, tokens, o_up2, o_up3, i_up2, i_up3, i_in, i_first, i_second, i_third = front(
        latent, cond[0], embed[0], audio_table[0], picks, out_proj[0], halves, splits, groups,
        per_device * HSIZE,
    )
    position = lax.axis_index("seq")
    block = position + jnp.arange(-2, 2)
    following = jnp.clip(block + 1, 0, devices - 1)
    inside = jnp.logical_and(block >= 0, block + 1 < devices)
    keep = jnp.where(jnp.logical_and(inside, tile_start[following] == 0), 1.0, 0.0)
    color = jnp.pad(flat(conv_color).T, ((0, 8 - conv_color.shape[3]), (0, 0)))
    gains = tuple(g[None] for g in (gain_first, gain_second, gain_third, gain_color))
    own = (halves[0], halves[1], o_up2, halves[3], o_up3, halves[5])
    other = (i_in, i_first, i_up2, i_second, i_up3, i_third)
    rgb = conv_color.shape[3]
    colors = decode(tokens, keep.astype(jnp.float32), color, gains, own, other, rgb)
    image = colors.reshape(rgb, 8, 8, -1).transpose(0, 1, 3, 2).reshape(rgb, 8, -1)
    return (handed[None], image)


def solution(mesh):
    in_specs = (
        P("section", ("replica", "seq"), None),
        P("section", None, ("replica", "seq"), None),
        P("section", None, None, None),
        P("section", "replica", None),
        P(("replica", "seq")),
        P("section", None, None),
        P("replica"),
        P(None, None, None, "section"),
        P(None, None, None, "section"),
        P(None, None, None, "section"),
        P(None, None, None, "section"),
        P(None, None, None, "section"),
        P(None, None, None, "section"),
        P(),
        P(),
        P(),
        P(),
        P(),
    )
    out_specs = (P("section", ("replica", "seq"), None), P(None, ("replica", "seq"), None))
    return jax.shard_map(body, mesh=mesh, in_specs=in_specs, out_specs=out_specs, check_vma=False)
```

profile of v0, /device:TPU:0, one launch (start us, length us, event | category | flops | bytes accessed | tf_op | source)
XLA Modules:
  0.0 110.3 jit_solution(10365745780794443461)
XLA Ops:
  0.6 0.0 copy-start
  0.6 0.0 copy-start.7
  0.7 0.0 copy-start.2
  0.7 0.0 copy-start.12
  0.7 0.0 copy-start.14
  0.7 0.0 copy-start.11
  0.7 0.0 copy-start.8
  0.7 1.2 %copy.27 = bf16[3,3,128,64]{3,2,1,0:T(8,128)(2,1)S(1)} copy(bf16[3,3,128,64]{2,3,1,0:T(8,128)(2,1)} %param.30) | data formatting | bytes 294912 | tf_op args[12]
  1.9 0.0 copy-start.1
  1.9 1.6 %copy.25 = bf16[1,4096,64]{2,1,0:T(8,128)(2,1)S(1)} copy(bf16[1,4096,64]{1,2,0:T(8,128)(2,1)} %param.23) | data formatting | bytes 1048576 | tf_op args[5]
  3.6 0.0 copy-done.12
  3.6 0.3 copy.26
  3.9 0.0 copy-done.14
  3.9 0.1 broadcast_in_dim.27
  4.0 0.1 eq.18
  4.1 0.1 fusion.picks
  4.1 0.0 copy-done.7
  4.2 0.0 copy-done.2
  4.2 0.0 copy-done.11
  4.2 0.0 copy-done.8
  4.2 0.0 copy-start.13
  4.2 58.1 %shard_map.185 = (f32[64,64]{1,0:T(8,128)S(1)}, bf16[5,64,64]{2,1,0:T(8,128)(2,1)S(1)}, bf16[4,2048,128]{2,1,0:T(8,128)(2,1)}, bf16[4,1024,64]{2,1,0:T(8,128)(2,...) custom-call(f32[64,64]{1,0:T(8,128)S(1)} %bitcast.33, ...), custom_call_target="tpu_custom_call" | custom-call | tf_op jit(solution)/shard_map/pallas_call | solution.py:296
  62.3 0.0 copy-done.1
  62.3 0.0 copy-start.3
  62.4 1.0 copy-done.3
  63.3 0.0 copy-start.4
  63.3 1.1 copy-done.4
  64.4 0.0 copy-start.5
  64.4 0.9 copy-done.5
  65.3 0.0 copy-start.6
  65.3 0.7 copy-done.6
  66.0 0.0 copy-start.9
  66.0 0.6 copy-done.9
  66.6 0.0 copy-start.10
  66.6 0.6 copy-done.10
  67.3 0.0 copy-done
  67.3 0.6 gather_fusion
  67.9 0.5 and_select_fusion.keep
  68.5 0.0 copy-done.13
  68.5 0.6 pad.4.w_color
  69.1 38.4 %shard_map.186 = f32[3,8,512]{2,1,0:T(8,128)} custom-call(f32[4]{0:T(128)} %and_select_fusion.keep, bf16[5,64,64]{2,1,0:T(8,128)(2,1)} %copy-done.9, bf16[8,1152]{1,0:T(8,128)(2,1)} %pad.4.w_color, f32[1,512]{1,0:T(1,128)} %bitcast.42, f32[1,256]{1,0:T(1,128)} %bitcast.43, f32[1,128]{1,0:T(1,128)} %bitcast.44, f32[1,128]{1,0:T(1,128)} %bitcast.45, ...), custom_call_target="tpu_custom_call" | custom-call | tf_op jit(solution)/shard_map/pallas_call | solution.py:534
  107.5 0.9 reshape.64
  108.4 0.3 copy.29
  108.6 1.0 reshape.65
  109.7 0.6 copy.31
  (2 shorter events, 0.0 us)
Async XLA Ops:
  0.6 66.6 %copy-start = (s32[8]{0:T(128)S(1)}, s32[8]{0:T(128)}, u32[]{:S(2)}) copy-start(s32[8]{0:T(128)} %param.24) | copy-start | bytes 100
  0.6 3.5 %copy-start.7 = (bf16[3,3,16,256]{3,2,1,0:T(8,128)(2,1)S(1)}, bf16[3,3,16,256]{3,2,1,0:T(8,128)(2,1)}, u32[]{:S(2)}) copy-start(bf16[3,3,16,256]{3,2,1,0:T(8,128)(2,1)} %param.25) | copy-start | bytes 221188
  0.7 3.5 %copy-start.2 = (bf16[3,3,256,128]{3,2,1,0:T(8,128)(2,1)S(1)}, bf16[3,3,256,128]{3,2,1,0:T(8,128)(2,1)}, u32[]{:S(2)}) copy-start(bf16[3,3,256,128]{3,2,1,0:T(8,128)(2,1)} %param.28) | copy-start | bytes 1769476
  0.7 2.9 %copy-start.12 = (bf16[3,3,256,64]{2,3,1,0:T(8,128)(2,1)S(1)}, bf16[3,3,256,64]{2,3,1,0:T(8,128)(2,1)}, u32[]{:S(2)}) copy-start(bf16[3,3,256,64]{2,3,1,0:T(8,128)(2,1)} %param.29) | copy-start | bytes 884740
  0.7 3.2 %copy-start.14 = (s32[4]{0:T(128)S(1)}, s32[4]{0:T(128)}, u32[]{:S(2)}) copy-start(s32[4]{0:T(128)} %param.22) | copy-start | bytes 52
  0.7 3.5 %copy-start.11 = (f32[1,64,64]{2,1,0:T(8,128)S(1)}, f32[1,64,64]{2,1,0:T(8,128)}, u32[]{:S(2)}) copy-start(f32[1,64,64]{2,1,0:T(8,128)} %param.18) | copy-start | bytes 49156
  0.7 3.5 %copy-start.8 = (bf16[1,32,4096]{2,1,0:T(8,128)(2,1)S(1)}, bf16[1,32,4096]{2,1,0:T(8,128)(2,1)}, u32[]{:S(2)}) copy-start(bf16[1,32,4096]{2,1,0:T(8,128)(2,1)} %param.21) | copy-start | bytes 786436
  1.9 60.4 %copy-start.1 = (bf16[3,3,128,64]{3,2,1,0:T(8,128)(2,1)}, bf16[3,3,128,64]{3,2,1,0:T(8,128)(2,1)S(1)}, u32[]{:S(2)}) copy-start(bf16[3,3,128,64]{3,2,1,0:T(8,128)(2,1)S(1)} %copy.27) | copy-start | bytes 442372
  4.2 64.3 %copy-start.13 = (bf16[3,3,128,3]{2,3,1,0:T(4,128)(2,1)S(1)}, bf16[3,3,128,3]{2,3,1,0:T(4,128)(2,1)}, u32[]{:S(2)}) copy-start(bf16[3,3,128,3]{2,3,1,0:T(4,128)(2,1)} %param.31) | copy-start | bytes 20740
  62.3 1.0 copy-start.3
  63.3 1.1 copy-start.4
  64.4 0.9 copy-start.5
  65.3 0.7 copy-start.6
  66.0 0.6 copy-start.9
  66.6 0.6 copy-start.10
where the time goes:
time: 111 us; the launch traced here: 110 us
  Pallas kernels  96.5 us (87%)
  local copies, waits for them, and re-layouts  12.3 us (11%)
    pallas_call x1, Pallas kernels, front(): pl.pallas_call(functools.partial(front_kernel, splits, heads_here, sectio...  58.1 us
    pallas_call x1, Pallas kernels, decode(): pl.pallas_call(decode_kernel, out_shape=jax.ShapeDtypeStruct((rgb, 8, 8 *...  38.4 us
    unnamed x34, local copies, waits for them, and re-layouts  8.71 us

commit v1 on v0

v1 whole, which is shorter than its diff:
```python
import functools
import math

import jax
import jax.numpy as jnp
from jax import lax
from jax.experimental import pallas as pl
from jax.experimental.pallas import tpu as pltpu
from jax.sharding import PartitionSpec as P

HEADS = 32
HSIZE = 128


step_size = -0.5
norm_eps = 1e-06


MESH = pl.DeviceIdType.MESH
F32, BF16 = jnp.float32, jnp.bfloat16
NT = (((1,), (1,)), ((), ()))


def lanes_of(shape):
    return lax.broadcasted_iota(jnp.int32, shape, len(shape) - 1)


def rows_of(shape):
    return lax.broadcasted_iota(jnp.int32, shape, len(shape) - 2)


def swap_halves(value):
    return pltpu.roll(value, value.shape[1] // 2, 1)


def dot(x, w):
    return jnp.dot(x, w, preferred_element_type=F32)


def scaled(value, factor):
    return value * lax.broadcast(factor, value.shape).astype(BF16)


def pairs(x, y, z):
    return ((x, y + z), (x + y, z))


def lift_second(raw, lifted):
    depth = raw.shape[1]
    chunk = 64

    @pl.loop(0, depth // chunk)
    def _(i):
        row = pl.multiple_of(i * chunk, chunk)
        w = [raw[t, pl.ds(row, chunk)].astype(F32) for t in range(9)]
        by_row = [pairs(w[q], w[3 + q], w[6 + q]) for q in range(3)]
        for a in (0, 1):
            for p in (0, 1):
                cols = pairs(*(by_row[q][a][p] for q in range(3)))
                for b in (0, 1):
                    for q in (0, 1):
                        at = pl.multiple_of((2 * p + q) * depth + row, chunk)
                        lifted[2 * a + b, pl.ds(at, chunk)] = cols[b][q].astype(BF16)


def lift_third_up(raw, lifted):
    outs, depth = raw.shape[1:]
    zero = jnp.zeros((depth, outs), BF16)
    w = [raw[t].astype(F32) for t in range(9)]
    by_row = [pairs(w[q], w[3 + q], w[6 + q]) for q in range(3)]
    for a in (0, 1):
        for p in (0, 1):
            cols = pairs(*(by_row[q][a][p] for q in range(3)))
            for b in (0, 1):
                for at in range(3):
                    inside = 0 <= at - b <= 1
                    block = cols[b][at - b].T.astype(BF16) if inside else zero
                    row = (3 * p + at) * depth
                    lifted[a, row : row + depth, b * outs : (b + 1) * outs] = block


def lift_third(raw, lifted):
    outs, depth = raw.shape[1:]
    zero = jnp.zeros((depth, outs), BF16)
    for r in range(3):
        for at in range(4):
            for e in (0, 1):
                inside = 0 <= at - e <= 2
                block = raw[3 * r + at - e].astype(F32).T.astype(BF16) if inside else zero
                row = (4 * r + at) * depth
                lifted[row : row + depth, e * outs : (e + 1) * outs] = block


def lift_input(raw, lifted, cell):
    chans = cell // 4
    zero = jnp.zeros((chans, raw.shape[1]), BF16)
    for a in (0, 1):
        for b in (0, 1):
            blocks = []
            for p in (0, 1):
                for q in (0, 1):
                    for i in (0, 1):
                        for j in (0, 1):
                            u, v = 2 * p + i - 1 + a, 2 * q + j - 1 + b
                            inside = 0 <= u <= 2 and 0 <= v <= 2
                            row = (3 * u + v) * chans
                            blocks.append(raw[row : row + chans] if inside else zero)
            lifted[2 * a + b] = jnp.concatenate(blocks, axis=0)


def lift_color(raw, lifted):
    color = raw[...].astype(F32)
    color = jnp.concatenate([color, jnp.zeros((8 - color.shape[0], color.shape[1]), F32)], axis=0)
    depth = color.shape[1] // 9
    zero = jnp.zeros((8, depth), F32)
    tile = lambda t: color[:, t * depth : (t + 1) * depth]
    for pair in range(4):
        blocks = []
        for f in (2 * pair, 2 * pair + 1):
            blocks.append(
                jnp.concatenate(
                    [
                        tile(3 * r + at - f) if 0 <= at - f <= 2 else zero
                        for r in range(3)
                        for at in range(10)
                    ],
                    axis=1,
                )
            )
        lifted[16 * pair : 16 * (pair + 1)] = jnp.concatenate(blocks, axis=0).astype(BF16)


def step_kernel(
    splits, per, chunk, sections, devices,
    amap, starts,
    latent, cond, embed, table, out_t,
    c_in, c_first, c_up2, c_second, c_up3, c_third, c_color, gain1, gain2, gain3, gain4,
    handed, image,
    lat, latd, xcat, condv, eq, ek, ev, wt, sq, skv, gq, gkv, acc, part, parts, resd, result,
    low, tokens, keep,
    r_in, w_first, r_up2, w_second, r_up3, r_third, r_color, g1, g2, g3, g4,
    w_in, w_up2, w_up3, w_third, w_color, order,
    a1, p1, x1, a2, p2, x2, a3, p3, p4, picture,
    in_sem, send_q, recv_q, send_kv, recv_kv, own_sem, send_p, recv_p,
    here_sem, send_w, recv_w, send_h, recv_h, send_r, recv_r, send_i, recv_i, out_sem, go,
):
    me = lax.axis_index("seq")
    section = lax.axis_index("section")
    last = section == sections - 1
    partner = {"section": lax.rem(section + 1, sections)}
    groups = devices // splits
    count, patch = lat.shape
    half = count // splits
    wide = chunk * HSIZE
    chunks = per // chunk
    my_group = me // splits
    cols = count

    tokens[...] = jnp.zeros(tokens.shape, BF16)
    barrier = pltpu.get_barrier_semaphore()
    for t in range(sections):

        @pl.loop(0, devices)
        def _(d):
            @pl.when(jnp.logical_or(d != me, section != t))
            def _():
                pl.semaphore_signal(
                    barrier, inc=1, device_id={"section": t, "seq": d}, device_id_type=MESH
                )

    frames = table.shape[0]
    loads = [
        pltpu.make_async_copy(src, dst, in_sem.at[k])
        for k, (src, dst) in enumerate(
            (
                (latent, lat), (embed.at[0], eq.at[pl.ds(0, patch)]),
                (table, eq.at[pl.ds(patch, frames)]), (embed.at[2], ev.at[pl.ds(0, patch)]),
                (table, ev.at[pl.ds(patch, frames)]), (embed.at[1], ek), (cond, condv),
                (out_t, wt), (gain1, g1), (gain2, g2), (gain3, g3), (gain4, g4),
                (c_color, r_color),
            )
        )
    ]
    for copy in loads:
        copy.start()

    weights = ((c_third, r_third), (c_in, r_in), (c_up3, r_up3), (c_up2, r_up2),
               (c_first, w_first), (c_second, w_second))

    def half_of(dst, k):
        if k in (0, 2):
            size = dst.shape[1] // 2
            return dst.at[:, pl.ds(pl.multiple_of(section * size, size), size)]
        size = dst.shape[-1] // 2
        lanes = pl.ds(pl.multiple_of(section * size, size), size)
        return dst.at[:, :, lanes] if len(dst.shape) == 3 else dst.at[:, lanes]

    mine = [
        pltpu.make_async_copy(src, half_of(dst, k), here_sem.at[k])
        for k, (src, dst) in enumerate(weights)
    ]
    given_w = [
        pltpu.make_async_remote_copy(
            src_ref=src, dst_ref=half_of(dst, k), send_sem=send_w.at[k], recv_sem=recv_w.at[k],
            device_id=partner, device_id_type=MESH,
        )
        for k, (src, dst) in enumerate(weights)
    ]

    blocks = starts.shape[0]

    def joined(by):
        block = me + by
        inside = jnp.logical_and(block >= 0, block + 1 < blocks)
        begins = starts[jnp.clip(block + 1, 0, blocks - 1)]
        return jnp.where(jnp.logical_and(inside, begins == 0), 1.0, 0.0).astype(F32)

    k_a, k_b, k_c, k_d = (joined(by) for by in (-2, -1, 0, 1))
    one = jnp.float32(1.0)
    upper = section == 0
    either = lambda x, y: jnp.where(upper, x, y)
    level1 = [either(x, y) for x, y in (
        (k_a, one), (one, k_b), (k_b, one), (one, k_c), (k_c, one), (one, k_d))]
    level2 = [either(x, y) for x, y in ((one, k_b), (k_b, one), (one, k_c), (k_c, one))]
    b_or, c_or = either(k_b, one), either(one, k_c)
    for k, value in enumerate(
        [k_a, k_b, k_c, k_d] + level1 + level2 + [one, b_or, one, c_or, one, one, one]
        + [b_or, one, c_or]
    ):
        keep[k] = value

    zrow = patch + frames
    eq[zrow:] = jnp.zeros((eq.shape[0] - zrow, eq.shape[1]), BF16)
    ev[zrow:] = jnp.zeros((ev.shape[0] - zrow, ev.shape[1]), BF16)
    perm_row = rows_of(order.shape)
    perm_col = lanes_of(order.shape)
    phase = lax.div(perm_row, jnp.int32(cols))
    target = (perm_row - phase * cols) * 8 + phase
    order[...] = jnp.where(perm_col == target, 1.0, 0.0).astype(BF16)

    loads[0].wait()
    latd[:, :patch] = lat[...]
    latd[:, patch:] = lat[...]
    row = rows_of(xcat.shape)
    lane = lanes_of(xcat.shape)
    per_block = count // amap.shape[0]
    frame = lax.broadcast(amap[0], xcat.shape)
    for k in range(1, amap.shape[0]):
        frame = jnp.where(row >= k * per_block, amap[k], frame)
    padded = latd[...]
    if xcat.shape[1] > padded.shape[1]:
        extra = xcat.shape[1] - padded.shape[1]
        padded = jnp.concatenate([padded, jnp.zeros((count, extra), F32)], axis=1)
    onehot = jnp.where(lane == frame + patch, 1.0, 0.0)
    xcat[...] = jnp.where(lane < patch, padded, onehot).astype(BF16)
    for copy in loads[1:8]:
        copy.wait()

    def q_copy(c, d, src):
        return pltpu.make_async_remote_copy(
            src_ref=sq.at[d // splits, c, pl.ds(lax.rem(d, splits) * half, half)],
            dst_ref=gq.at[c, pl.ds(src * half, half)],
            send_sem=send_q.at[c, d], recv_sem=recv_q.at[c, src],
            device_id={"seq": d}, device_id_type=MESH,
        )

    def kv_copy(c, d, src):
        return pltpu.make_async_remote_copy(
            src_ref=skv.at[d // splits, c],
            dst_ref=gkv.at[c, pl.ds(src * count, count)],
            send_sem=send_kv.at[c, d], recv_sem=recv_kv.at[c, src],
            device_id={"seq": d}, device_id_type=MESH,
        )

    near = max(groups // 2, 1)

    def turn(k):
        side = lax.rem(my_group // near + 1 + k // near, max(groups // near, 1))
        return side * near + lax.rem(my_group + 1 + lax.rem(k, near), near)

    def send(c, g):
        @pl.loop(0, splits)
        def _(r):
            d = g * splits + r

            @pl.when(d != me)
            def _():
                q_copy(c, d, me).start()
                kv_copy(c, d, me).start()

    pl.semaphore_wait(barrier, sections * devices - 1)
    for copy in given_w[:2]:
        copy.start()
    for copy in mine:
        copy.start()

    for c in range(chunks):

        @pl.loop(0, groups)
        def _(k):
            g = turn(k)
            at = pl.ds(pl.multiple_of(g * (per * HSIZE) + c * wide, HSIZE), wide)
            q = dot(xcat[...], eq[:, at]) + condv[0, :, at].astype(F32)
            key = dot(xcat[:, :patch], ek[:, at]) + condv[1, :, at].astype(F32)
            v = dot(xcat[...], ev[:, at]) + condv[2, :, at].astype(F32)
            w = wt[:, at]
            if chunk == 2:
                first = lanes_of(w.shape) < HSIZE
                zero = jnp.zeros(w.shape, BF16)
                w = jnp.concatenate([jnp.where(first, w, zero), jnp.where(first, zero, w)], axis=0)
            else:
                w = jnp.concatenate([w, jnp.zeros((128 - w.shape[0], w.shape[1]), BF16)], axis=0)
            mixed = lax.dot_general(v.astype(BF16), w, NT, preferred_element_type=F32)
            sq[g, c] = q.astype(BF16)
            skv[g, c, :, :wide] = key.astype(BF16)
            skv[g, c, :, wide:] = mixed.astype(BF16)

            @pl.when(last)
            def _():
                send(c, g)

    for copy in given_w[2:]:
        copy.start()

    own = []
    for c in range(chunks):
        own.append(pltpu.make_async_copy(
            sq.at[my_group, c, pl.ds(lax.rem(me, splits) * half, half)],
            gq.at[c, pl.ds(me * half, half)], own_sem.at[c, 0],
        ))
        own.append(pltpu.make_async_copy(
            skv.at[my_group, c], gkv.at[c, pl.ds(me * count, count)], own_sem.at[c, 1]
        ))
    for copy in own:
        copy.start()

    for copy in loads[8:]:
        copy.wait()
    lift_color(r_color, w_color)
    mine[0].wait()
    given_w[0].wait_recv()
    lift_third(r_third, w_third)
    mine[1].wait()
    given_w[1].wait_recv()
    lift_input(r_in, w_in, patch)
    mine[2].wait()
    given_w[2].wait_recv()
    lift_third_up(r_up3, w_up3)
    mine[3].wait()
    given_w[3].wait_recv()
    lift_second(r_up2, w_up2)

    queries = gq.shape[1]
    block = min(256, queries)
    parts_of = queries // block
    scale = 1.0 / math.sqrt(HSIZE)
    lane128 = lanes_of((block, 128))
    both = half // 2

    def attend(c):
        own[2 * c].wait()
        own[2 * c + 1].wait()

        @pl.loop(0, devices)
        def _(d):
            @pl.when(d != me)
            def _():
                q_copy(c, d, d).wait_recv()
                kv_copy(c, d, d).wait_recv()

        @pl.loop(0, parts_of)
        def _(i):
            at = pl.ds(pl.multiple_of(i * block, block), block)
            outs = []
            for h in range(chunk):
                own_lanes = slice(h * HSIZE, (h + 1) * HSIZE)
                scores = lax.dot_general(
                    gq[c, at, own_lanes], gkv[c, :, own_lanes], NT, preferred_element_type=F32
                ) * scale
                top = jnp.max(scores, axis=1, keepdims=True)
                weights_h = jnp.exp(scores - top)
                total = jnp.sum(weights_h, axis=1, keepdims=True)
                outs.append(dot(weights_h.astype(BF16), gkv[c, :, wide:]) / total)
            value = outs[0] if chunk == 1 else jnp.where(lane128 < patch, outs[0], outs[1])
            if c > 0:
                value = value + acc[at]
            if c < chunks - 1:
                acc[at] = value
            else:
                value = value + swap_halves(value)
                for k in range(block // half):
                    low_rows = value[k * half : k * half + both]
                    high_rows = value[k * half + both : (k + 1) * half]
                    first = lanes_of(low_rows.shape) < patch
                    part[i * (block // half) + k] = jnp.where(first, low_rows, high_rows)

    def part_copy(d, src):
        return pltpu.make_async_remote_copy(
            src_ref=part.at[d], dst_ref=parts.at[src],
            send_sem=send_p.at[d], recv_sem=recv_p.at[src],
            device_id={"seq": d}, device_id_type=MESH,
        )

    def send_parts():
        @pl.loop(1, devices)
        def _(k):
            part_copy(lax.rem(me + k, devices), me).start()

    def settle():
        @pl.loop(0, devices)
        def _(d):
            @pl.when(d != me)
            def _():
                part_copy(d, d).wait_recv()

        for r in range(splits):
            total = jnp.zeros((both, 128), F32)
            for g in range(groups):
                d = g * splits + r
                total = total + jnp.where(d == me, part[d], parts[d])
            first = lanes_of(total.shape) < patch
            other = swap_halves(total)
            at = r * half
            low_rows = jnp.where(first, total, other)
            high_rows = jnp.where(first, other, total)
            resd[at : at + both] = latd[at : at + both] + step_size * low_rows
            resd[at + both : at + half] = latd[at + both : at + half] + step_size * high_rows
        result[...] = resd[:, :patch]

    given = pltpu.make_async_remote_copy(
        src_ref=result, dst_ref=handed, send_sem=send_r, recv_sem=recv_r,
        device_id=partner, device_id_type=MESH,
    )

    def row_copy(by, t, to):
        return pltpu.make_async_remote_copy(
            src_ref=low, dst_ref=tokens.at[2 - by],
            send_sem=send_h.at[2 - by, t], recv_sem=recv_h.at[2 - by],
            device_id={"section": t, "seq": lax.rem(to + devices, devices)}, device_id_type=MESH,
        )

    side_copy = pltpu.make_async_remote_copy(
        src_ref=low, dst_ref=tokens.at[2], send_sem=send_h.at[2, 0], recv_sem=recv_h.at[2],
        device_id=partner, device_id_type=MESH,
    )

    def inside(by):
        return jnp.logical_and(me + by >= 0, me + by < devices)

    def sent_all():
        @pl.loop(0, devices)
        def _(d):
            @pl.when(d != me)
            def _():
                for c in range(chunks):
                    q_copy(c, d, me).wait_send()
                    kv_copy(c, d, me).wait_send()

    @pl.when(last)
    def _():
        for c in range(chunks):
            if c == chunks - 1:
                sent_all()
                pl.semaphore_signal(go, inc=1, device_id=partner, device_id_type=MESH)
            attend(c)
        send_parts()
        settle()
        low[...] = resd[...].astype(BF16)
        for by in (1, -1, 2, -2):
            for t in range(sections):

                @pl.when(inside(by))
                def _():
                    row_copy(by, t, me + by).start()

        side_copy.start()
        given.start()
        tokens[2] = low[...]

    @pl.when(jnp.logical_not(last))
    def _():
        pl.semaphore_wait(go, 1)
        for c in range(chunks):

            @pl.loop(0, groups)
            def _(k):
                send(c, turn(k))

        side_copy.wait_recv()

    for by in (1, -1, 2, -2):

        @pl.when(inside(-by))
        def _():
            row_copy(by, 0, me - by).wait_recv()

    def moved(value, by):
        position = rows_of(value.shape)
        if by > 0:
            return jnp.where(position > 0, pltpu.roll(value, 1, 0), 0.0)
        return jnp.where(position < cols - 1, pltpu.roll(value, cols - 1, 0), 0.0)

    def put(buf, index, value):
        phases = value.shape[0]
        buf[index, 1 : phases + 1] = value.astype(BF16)
        buf[index, 0] = moved(value[phases - 1], 1).astype(BF16)
        buf[index, phases + 1] = moved(value[0], -1).astype(BF16)

    def act(value, gain):
        square = jnp.mean(value * value, axis=-1, keepdims=True)
        h = value * (0.5 * lax.rsqrt(square + norm_eps)) * gain[...]
        return h + h * jnp.tanh(h)

    def flat(value):
        return value.reshape(-1, value.shape[-1])

    cells = []
    for i in range(5):
        value = tokens[i].astype(F32)
        first = lanes_of(value.shape) < patch
        cells.append((
            jnp.where(first, moved(value, 1), value).astype(BF16),
            jnp.where(first, value, moved(value, -1)).astype(BF16),
        ))
    for a in (0, 1):
        for b in (0, 1):
            x = []
            for j in range(4):
                above, below = cells[j][b], cells[j + 1][b]
                if a == 0:
                    above = scaled(above, keep[j])
                else:
                    below = scaled(below, keep[j])
                x.append(jnp.concatenate([above, below], axis=1))
            y = dot(jnp.concatenate(x, axis=0), w_in[2 * a + b]).astype(BF16)
            for j in range(4):
                a1[2 * j + 1 - a, b] = y[j * cols : (j + 1) * cols]

    shift = section

    @pl.loop(0, 7)
    def _(i):
        put(p1, i, act(a1[i + shift].astype(F32), g1))

    mine[4].wait()
    given_w[4].wait_recv()
    outs1 = w_first.shape[1] // 2
    for n in range(2):
        taps = []
        for p in range(3):
            for q in range(3):
                piece = []
                for j in range(5):
                    value = p1[j + p, q : q + 2]
                    if p == 0:
                        value = scaled(value, keep[4 + j])
                    elif p == 2:
                        value = scaled(value, keep[5 + j])
                    piece.append(flat(value))
                taps.append(jnp.concatenate(piece, axis=0))
        lanes = slice(n * outs1, (n + 1) * outs1)
        y = dot(jnp.concatenate(taps, axis=1), w_first[:, lanes])
        for j in range(5):
            base = a1[j + 1 + shift, :, :, lanes]
            value = base.astype(F32) + y[2 * j * cols : 2 * (j + 1) * cols].reshape(base.shape)
            x1[j, 1:3, :, lanes] = value.astype(BF16)
            x1[j, 0, :, lanes] = moved(value[1], 1).astype(BF16)
            x1[j, 3, :, lanes] = moved(value[0], -1).astype(BF16)

    @pl.loop(0, 4)
    def _(k):
        a, b = k // 2, lax.rem(k, 2)
        taps = []
        for p in (0, 1):
            for q in (0, 1):
                piece = []
                for j in range(4):
                    value = x1[j + p, pl.ds(b + q, 2)]
                    factor = jnp.where(a == p, keep[5 + j], 1.0)
                    piece.append(flat(scaled(value, factor)))
                taps.append(jnp.concatenate(piece, axis=0))
        y = dot(jnp.concatenate(taps, axis=1), w_up2[k]).astype(BF16)
        for j in range(4):
            for f in (0, 1):
                at = (2 * j + f) * cols
                a2[2 * j + 1 - a, 2 * f + b] = y[at : at + cols]

    @pl.when(jnp.logical_not(last))
    def _():
        for c in range(chunks):
            attend(c)
        send_parts()

    @pl.loop(0, 8)
    def _(i):
        put(p2, i, act(a2[i].astype(F32), g2))

    mine[5].wait()
    given_w[5].wait_recv()

    @pl.loop(0, 3)
    def _(t):
        taps = []
        for p in range(3):
            for q in range(3):
                piece = []
                for j in range(2):
                    value = p2[2 * t + j + p, q : q + 4]
                    if (p, j) == (0, 0):
                        value = scaled(value, keep[10 + t])
                    elif (p, j) == (2, 1):
                        value = scaled(value, keep[11 + t])
                    piece.append(flat(value))
                taps.append(jnp.concatenate(piece, axis=0))
        y = dot(jnp.concatenate(taps, axis=1), w_second[...])
        for j in range(2):
            base = a2[2 * t + 1 + j]
            put(x2, 2 * t + j,
                base.astype(F32) + y[4 * j * cols : 4 * (j + 1) * cols].reshape(base.shape))

    @pl.when(jnp.logical_not(last))
    def _():
        settle()
        given.start()

    @pl.loop(0, 2)
    def _(a):
        taps = []
        for p in (0, 1):
            for q in range(3):
                piece = []
                for j in range(4):
                    value = x2[j + a + p, q : q + 4]
                    factor = jnp.where(a == p, keep[14 + j + a], 1.0)
                    piece.append(flat(scaled(value, factor)))
                taps.append(jnp.concatenate(piece, axis=0))
        y = dot(jnp.concatenate(taps, axis=1), w_up3[a]).astype(BF16)
        outs3 = a3.shape[-1]
        for j in range(4):
            for f in range(4):
                at = (4 * j + f) * cols
                for b in (0, 1):
                    a3[2 * j + a, 2 * f + b] = y[at : at + cols, b * outs3 : (b + 1) * outs3]

    @pl.loop(0, 8)
    def _(i):
        put(p3, i, act(a3[i].astype(F32), g3))

    @pl.loop(0, 3)
    def _(t):
        taps = []
        for p in range(3):
            for q in range(4):
                piece = []
                for j in range(2):
                    for e in range(4):
                        value = p3[2 * t + j + p, 2 * e + q]
                        if (p, j) == (2, 0) or (p, j) == (0, 1):
                            value = scaled(value, keep[21 + t])
                        piece.append(value)
                taps.append(jnp.concatenate(piece, axis=0))
        y = dot(jnp.concatenate(taps, axis=1), w_third[...])
        outs3 = a3.shape[-1]
        for j in range(2):
            value = jnp.stack([
                y[(4 * j + f // 2) * cols : (4 * j + f // 2 + 1) * cols,
                  (f % 2) * outs3 : (f % 2 + 1) * outs3]
                for f in range(8)
            ])
            value = (a3[2 * t + 1 + j].astype(F32) + value).astype(BF16).astype(F32)
            put(p4, 2 * t + j, act(value, g4))

    p4[0] = scaled(p4[0], keep[21])
    p4[5] = scaled(p4[5], keep[23])
    window = jnp.concatenate(
        [
            jnp.concatenate([p4[s + r, at] for s in range(4)], axis=0)
            for r in range(3)
            for at in range(10)
        ],
        axis=1,
    )
    colors = lax.dot_general(w_color[...], window, NT, preferred_element_type=F32)
    lines = []
    for s in range(4):
        line = []
        for pair in range(4):
            lanes = slice((s // 2) * 128, (s // 2 + 1) * 128)
            even = colors[16 * pair : 16 * pair + 8, lanes]
            odd = colors[16 * pair + 8 : 16 * pair + 16, lanes]
            first = lanes_of(even.shape) < cols
            if s % 2 == 0:
                line.append(jnp.where(first, even, swap_halves(odd)))
            else:
                line.append(jnp.where(first, swap_halves(even), odd))
        lines.append(jnp.concatenate(line, axis=1))
    value = jnp.concatenate(lines, axis=0)
    high = value.astype(BF16)
    rest = value - high.astype(F32)
    middle = rest.astype(BF16)
    final = (rest - middle.astype(F32)).astype(BF16)
    placed = dot(jnp.concatenate([high, middle, final], axis=0), order[...])
    placed = placed[:32] + (placed[32:64] + placed[64:])
    for k in range(picture.shape[0]):
        for s in range(4):
            picture[k, s : s + 1] = placed[8 * s + k : 8 * s + k + 1]

    shown = pltpu.make_async_copy(picture, image.at[section], out_sem)
    shared = pltpu.make_async_remote_copy(
        src_ref=picture, dst_ref=image.at[section], send_sem=send_i, recv_sem=recv_i,
        device_id=partner, device_id_type=MESH,
    )
    shared.start()
    shown.start()

    given.wait_recv()
    given.wait_send()

    @pl.when(last)
    def _():
        side_copy.wait_send()
        for by in (1, -1, 2, -2):
            for t in range(sections):

                @pl.when(inside(by))
                def _():
                    row_copy(by, t, me + by).wait_send()

    @pl.when(jnp.logical_not(last))
    def _():
        sent_all()

    @pl.loop(0, devices)
    def _(d):
        @pl.when(d != me)
        def _():
            part_copy(d, me).wait_send()

    for copy in given_w:
        copy.wait_send()
    shown.wait()
    shared.wait()


def body(
    latents, cond, embed, audio_table, audio_map, out_proj, tile_start,
    conv_input, conv_first, conv_second_up, conv_second, conv_third_up, conv_third, conv_color,
    gain_first, gain_second, gain_third, gain_color,
):
    devices, sections = lax.axis_size("seq"), lax.axis_size("section")
    splits = max(devices // HEADS, 1)
    per = max(HEADS // devices, 1)
    groups = devices // splits
    chunk = 2 if per % 2 == 0 else 1
    chunks = per // chunk
    wide = chunk * HSIZE
    latent = latents[0]
    count, patch = latent.shape
    half = count // splits
    features = cond.shape[-1]
    depth = -(-(patch + audio_table.shape[1]) // 128) * 128
    flat = lambda w: w.reshape(-1, w.shape[-1])
    taps = lambda w: w.reshape(9, *w.shape[2:])
    turned = lambda w: taps(jnp.swapaxes(w, 2, 3))
    c1, c2 = 2 * conv_first.shape[3], 2 * conv_second.shape[3]
    c3 = 2 * conv_third.shape[3]
    rgb = conv_color.shape[3]
    vmem = lambda shape, kind=BF16: pltpu.VMEM(shape, kind)
    dma = pltpu.SemaphoreType.DMA
    hbm = pl.BlockSpec(memory_space=pl.ANY)
    smem = pl.BlockSpec(memory_space=pltpu.SMEM)
    operands = (
        audio_map, tile_start,
        latent, cond[0], embed[0], audio_table[0], out_proj[0].T,
        flat(conv_input), flat(conv_first), taps(conv_second_up), flat(conv_second),
        turned(conv_third_up), turned(conv_third), flat(conv_color).T,
        gain_first[None], gain_second[None], gain_third[None], gain_color[None],
    )
    handed, image = pl.pallas_call(
        functools.partial(step_kernel, splits, per, chunk, sections, devices),
        out_shape=(
            jax.ShapeDtypeStruct(latent.shape, F32),
            jax.ShapeDtypeStruct((2, rgb, 4, 8 * count), F32),
        ),
        in_specs=[smem] * 2 + [hbm] * (len(operands) - 2),
        out_specs=(hbm, hbm),
        scratch_shapes=[
            vmem((count, patch), F32), vmem((count, 2 * patch), F32), vmem((count, depth)),
            vmem((3, count, features)), vmem((depth, features)), vmem((patch, features)),
            vmem((depth, features)), vmem((patch, features)),
            vmem((groups, chunks, count, wide)), vmem((groups, chunks, count, wide + 128)),
            vmem((chunks, devices * half, wide)), vmem((chunks, devices * count, wide + 128)),
            vmem((devices * half, 128), F32),
            vmem((devices, half // 2, 128), F32), vmem((devices, half // 2, 128), F32),
            vmem((count, 2 * patch), F32), vmem((count, patch), F32),
            vmem((count, 2 * patch)), vmem((5, count, 2 * patch)),
            pltpu.SMEM((24,), F32),
            vmem((9 * patch // 4, c1)), vmem((9 * c1, c1)), vmem((9, c1, c2)),
            vmem((9 * c2, c2)), vmem((9, c3, c2)), vmem((9, c3, c3)), vmem((rgb, 9 * c3)),
            vmem((1, c1), F32), vmem((1, c2), F32), vmem((1, c3), F32), vmem((1, c3), F32),
            vmem((4, 4 * patch, c1)), vmem((4, 4 * c1, c2)), vmem((2, 6 * c2, 2 * c3)),
            vmem((12 * c3, 2 * c3)), vmem((64, 30 * c3)), vmem((8 * count, 8 * count)),
            vmem((8, 2, count, c1)), vmem((7, 4, count, c1)), vmem((5, 4, count, c1)),
            vmem((8, 4, count, c2)), vmem((8, 6, count, c2)), vmem((6, 6, count, c2)),
            vmem((8, 8, count, c3)), vmem((8, 10, count, c3)), vmem((6, 10, count, c3)),
            vmem((rgb, 4, 8 * count), F32),
            dma((13,)), dma((chunks, devices)), dma((chunks, devices)),
            dma((chunks, devices)), dma((chunks, devices)), dma((chunks, 2)),
            dma((devices,)), dma((devices,)), dma((6,)), dma((6,)), dma((6,)),
            dma((5, sections)), dma((5,)), dma, dma, dma, dma, dma,
            pltpu.SemaphoreType.REGULAR,
        ],
        compiler_params=pltpu.CompilerParams(
            collective_id=0, has_side_effects=True, vmem_limit_bytes=60 * 1024 * 1024
        ),
    )(*operands)
    image = jnp.swapaxes(image, 0, 1).reshape(rgb, 8, 8 * count)
    return (handed[None], image)


def solution(mesh):
    in_specs = (
        P("section", ("replica", "seq"), None),
        P("section", None, ("replica", "seq"), None),
        P("section", None, None, None),
        P("section", "replica", None),
        P(("replica", "seq")),
        P("section", None, None),
        P("replica"),
        P(None, None, None, "section"),
        P(None, None, None, "section"),
        P(None, None, None, "section"),
        P(None, None, None, "section"),
        P(None, None, None, "section"),
        P(None, None, None, "section"),
        P(),
        P(),
        P(),
        P(),
        P(),
    )
    out_specs = (P("section", ("replica", "seq"), None), P(None, ("replica", "seq"), None))
    return jax.shard_map(body, mesh=mesh, in_specs=in_specs, out_specs=out_specs, check_vma=False)
```

time: 111 us -> 62.5 us (0.56)
  Pallas kernels: 96.5 us -> 58.8 us
  local copies, waits for them, and re-layouts: 12.3 us -> 2.82 us
    pallas_call x2 -> x1, Pallas kernels: 96.5 us -> 58.8 us  [body(): pl.pallas_call(functools.partial(step_kernel, splits, per, chunk, section...]
    unnamed x34 -> x1, local copies, waits for them, and re-layouts: 8.71 us -> 1.37 us
    reshape x3 -> x1, local copies, waits for them, and re-layouts: 2.17 us -> 0.64 us  [body(): image = jnp.swapaxes(image, 0, 1).reshape(rgb, 8, 8 * count)]
where the time goes in v1:
time: 62.5 us; the launch traced here: 62.2 us
  Pallas kernels  58.8 us (94%)
  local copies, waits for them, and re-layouts  2.82 us (5%)
  between operations  0.65 us (1%)
    pallas_call x1, Pallas kernels, body(): pl.pallas_call(functools.partial(step_kernel, splits, per, chunk, section...  58.8 us
    unnamed x1, local copies, waits for them, and re-layouts  1.37 us

profile of v1, /device:TPU:0, one launch (start us, length us, event | category | flops | bytes accessed | tf_op | source)
XLA Modules:
  0.0 62.2 jit_solution(950774932228583463)
XLA Ops:
  0.6 58.8 %shard_map.185 = (f32[64,64]{1,0:T(8,128)}, f32[2,3,4,512]{3,2,1,0:T(4,128)}) custom-call(s32[4]{0:T(128)} %amap.1, s32[8]{0:T(128)} %starts.1, f32[64,64]{1,0:T(8,128)} %bitcast.37, bf16[3,64,4096]{2,1,0:T(8,128)(2,1)} %bitcast.27, bf16[3,64,4096]{2,1,0:T(8,128)(2,1)} %bitcast.28, bf16[32,4096]{1,0:T(8,128)(2,1)} %bitcast.33, bf16[64,4096]{1,0:T(8,128)(2,1)} %bitcast.31, ...), custom_call_target="tpu_custom_call" | custom-call | tf_op jit(solution)/shard_map/pallas_call | solution.py:779
  59.4 0.8 %copy.22 = f32[3,2,4,512]{3,2,1,0:T(4,128)S(1)} copy(f32[3,2,4,512]{3,2,0,1:T(4,128)} %bitcast.36) | data formatting | bytes 98304 | tf_op jit(solution)/shard_map/transpose | solution.py:817
  60.2 0.6 %reshape.35 = f32[3,8,512]{2,1,0:T(8,128)} reshape(f32[3,2,4,512]{3,2,1,0:T(4,128)S(1)} %copy.22) | data formatting | bytes 98304 | tf_op jit(solution)/shard_map/reshape | solution.py:817
  60.8 1.4 %copy.24 = f32[1,64,64]{2,1,0:T(8,128)} copy(f32[1,64,64]{2,1,0:T(8,128)} %bitcast.38) | data formatting | bytes 32768

commit v2 on v1

--- a/solution.py
+++ b/solution.py
@@ -159,14 +159,14 @@
     tokens[...] = jnp.zeros(tokens.shape, BF16)
     barrier = pltpu.get_barrier_semaphore()
     for t in range(sections):
-
-        @pl.loop(0, devices)
-        def _(d):
-            @pl.when(jnp.logical_or(d != me, section != t))
-            def _():
-                pl.semaphore_signal(
-                    barrier, inc=1, device_id={"section": t, "seq": d}, device_id_type=MESH
-                )
+        peer = lax.rem(section + t, sections)
+
+        @pl.loop(0 if t else 1, devices)
+        def _(k):
+            d = lax.rem(me + k, devices)
+            pl.semaphore_signal(
+                barrier, inc=1, device_id={"section": peer, "seq": d}, device_id_type=MESH
+            )
 
     frames = table.shape[0]
     loads = [
@@ -273,10 +273,14 @@
         )
 
     near = max(groups // 2, 1)
+    quarter = max(groups // 4, 1)
+    inner = lax.rem((my_group // quarter + 1) // 2, 2)
 
     def turn(k):
-        side = lax.rem(my_group // near + 1 + k // near, max(groups // near, 1))
+        side = lax.rem(my_group // near + inner + k // near, max(groups // near, 1))
         return side * near + lax.rem(my_group + 1 + lax.rem(k, near), near)
+
+    sharp = math.log2(math.e) / math.sqrt(HSIZE)
 
     def send(c, g):
         @pl.loop(0, splits)
@@ -353,7 +357,6 @@
     queries = gq.shape[1]
     block = min(256, queries)
     parts_of = queries // block
-    scale = 1.0 / math.sqrt(HSIZE)
     lane128 = lanes_of((block, 128))
     both = half // 2
 
@@ -376,11 +379,12 @@
                 own_lanes = slice(h * HSIZE, (h + 1) * HSIZE)
                 scores = lax.dot_general(
                     gq[c, at, own_lanes], gkv[c, :, own_lanes], NT, preferred_element_type=F32
-                ) * scale
+                ) * sharp
                 top = jnp.max(scores, axis=1, keepdims=True)
-                weights_h = jnp.exp(scores - top)
-                total = jnp.sum(weights_h, axis=1, keepdims=True)
-                outs.append(dot(weights_h.astype(BF16), gkv[c, :, wide:]) / total)
+                values = gkv[c, :, wide:]
+                values = jnp.concatenate([values, jnp.ones(values.shape, BF16)], axis=1)
+                summed = dot(jnp.exp2(scores - top).astype(BF16), values)
+                outs.append(summed[:, :128] / summed[:, 128:])
             value = outs[0] if chunk == 1 else jnp.where(lane128 < patch, outs[0], outs[1])
             if c > 0:
                 value = value + acc[at]
@@ -538,8 +542,7 @@
 
     shift = section
 
-    @pl.loop(0, 7)
-    def _(i):
+    for i in range(7):
         put(p1, i, act(a1[i + shift].astype(F32), g1))
 
     mine[4].wait()
@@ -567,17 +570,15 @@
             x1[j, 0, :, lanes] = moved(value[1], 1).astype(BF16)
             x1[j, 3, :, lanes] = moved(value[0], -1).astype(BF16)
 
-    @pl.loop(0, 4)
-    def _(k):
-        a, b = k // 2, lax.rem(k, 2)
+    for k in range(4):
+        a, b = k // 2, k % 2
         taps = []
         for p in (0, 1):
             for q in (0, 1):
                 piece = []
                 for j in range(4):
-                    value = x1[j + p, pl.ds(b + q, 2)]
-                    factor = jnp.where(a == p, keep[5 + j], 1.0)
-                    piece.append(flat(scaled(value, factor)))
+                    value = x1[j + p, b + q : b + q + 2]
+                    piece.append(flat(scaled(value, keep[5 + j]) if a == p else value))
                 taps.append(jnp.concatenate(piece, axis=0))
         y = dot(jnp.concatenate(taps, axis=1), w_up2[k]).astype(BF16)
         for j in range(4):
@@ -585,21 +586,13 @@
                 at = (2 * j + f) * cols
                 a2[2 * j + 1 - a, 2 * f + b] = y[at : at + cols]
 
-    @pl.when(jnp.logical_not(last))
-    def _():
-        for c in range(chunks):
-            attend(c)
-        send_parts()
-
-    @pl.loop(0, 8)
-    def _(i):
+    for i in range(8):
         put(p2, i, act(a2[i].astype(F32), g2))
 
     mine[5].wait()
     given_w[5].wait_recv()
 
-    @pl.loop(0, 3)
-    def _(t):
+    for t in range(3):
         taps = []
         for p in range(3):
             for q in range(3):
@@ -620,19 +613,20 @@
 
     @pl.when(jnp.logical_not(last))
     def _():
-        settle()
-        given.start()
-
-    @pl.loop(0, 2)
-    def _(a):
+        for c in range(chunks):
+            attend(c)
+        send_parts()
+
+    for a in range(2):
         taps = []
         for p in (0, 1):
             for q in range(3):
                 piece = []
                 for j in range(4):
                     value = x2[j + a + p, q : q + 4]
-                    factor = jnp.where(a == p, keep[14 + j + a], 1.0)
-                    piece.append(flat(scaled(value, factor)))
+                    if a == p and j + a in (1, 3):
+                        value = scaled(value, keep[14 + j + a])
+                    piece.append(flat(value))
                 taps.append(jnp.concatenate(piece, axis=0))
         y = dot(jnp.concatenate(taps, axis=1), w_up3[a]).astype(BF16)
         outs3 = a3.shape[-1]
@@ -642,12 +636,15 @@
                 for b in (0, 1):
                     a3[2 * j + a, 2 * f + b] = y[at : at + cols, b * outs3 : (b + 1) * outs3]
 
-    @pl.loop(0, 8)
-    def _(i):
+    for i in range(8):
         put(p3, i, act(a3[i].astype(F32), g3))
 
-    @pl.loop(0, 3)
-    def _(t):
+    @pl.when(jnp.logical_not(last))
+    def _():
+        settle()
+        given.start()
+
+    for t in range(3):
         taps = []
         for p in range(3):
             for q in range(4):
@@ -655,7 +652,7 @@
                 for j in range(2):
                     for e in range(4):
                         value = p3[2 * t + j + p, 2 * e + q]
-                        if (p, j) == (2, 0) or (p, j) == (0, 1):
+                        if t != 1 and (p, j) in ((2, 0), (0, 1)):
                             value = scaled(value, keep[21 + t])
                         piece.append(value)
                 taps.append(jnp.concatenate(piece, axis=0))
@@ -742,6 +739,12 @@
     shared.wait()
 
 
+def finish_kernel(handed, image, handed_out, image_out):
+    handed_out[...] = handed[...]
+    for s in range(2):
+        image_out[:, 4 * s : 4 * s + 4] = image[s]
+
+
 def body(
     latents, cond, embed, audio_table, audio_map, out_proj, tile_start,
     conv_input, conv_first, conv_second_up, conv_second, conv_third_up, conv_third, conv_color,
@@ -769,6 +772,7 @@
     dma = pltpu.SemaphoreType.DMA
     hbm = pl.BlockSpec(memory_space=pl.ANY)
     smem = pl.BlockSpec(memory_space=pltpu.SMEM)
+    whole = pl.BlockSpec(memory_space=pltpu.VMEM)
     operands = (
         audio_map, tile_start,
         latent, cond[0], embed[0], audio_table[0], out_proj[0].T,
@@ -783,7 +787,7 @@
             jax.ShapeDtypeStruct((2, rgb, 4, 8 * count), F32),
         ),
         in_specs=[smem] * 2 + [hbm] * (len(operands) - 2),
-        out_specs=(hbm, hbm),
+        out_specs=(whole, whole),
         scratch_shapes=[
             vmem((count, patch), F32), vmem((count, 2 * patch), F32), vmem((count, depth)),
             vmem((3, count, features)), vmem((depth, features)), vmem((patch, features)),
@@ -814,7 +818,15 @@
             collective_id=0, has_side_effects=True, vmem_limit_bytes=60 * 1024 * 1024
         ),
     )(*operands)
-    image = jnp.swapaxes(image, 0, 1).reshape(rgb, 8, 8 * count)
+    handed, image = pl.pallas_call(
+        finish_kernel,
+        out_shape=(
+            jax.ShapeDtypeStruct(latent.shape, F32),
+            jax.ShapeDtypeStruct((rgb, 8, 8 * count), F32),
+        ),
+        in_specs=[whole, whole],
+        out_specs=(whole, whole),
+    )(handed, image)
     return (handed[None], image)
 
 

time: 62.5 us -> 58.9 us (0.942)
  local copies, waits for them, and re-layouts: 2.82 us -> 0 us
  Pallas kernels: 58.8 us -> 58.1 us
    pallas_call x1, Pallas kernels: 58.8 us -> 56.6 us  [body(): pl.pallas_call(functools.partial(step_kernel, splits, per, chunk, section...]
    pallas_call x0 -> x1, Pallas kernels: none -> 1.45 us  [body(): pl.pallas_call(finish_kernel, out_shape=(jax.ShapeDtypeStruct(latent.shap...]
    unnamed x1 -> x0, local copies, waits for them, and re-layouts: 1.37 us -> none
    transpose x1 -> x0, local copies, waits for them, and re-layouts: 0.8 us -> none  [body(): image = jnp.swapaxes(image, 0, 1).reshape(rgb, 8, 8 * count)]
    reshape x1 -> x0, local copies, waits for them, and re-layouts: 0.64 us -> none  [body(): image = jnp.swapaxes(image, 0, 1).reshape(rgb, 8, 8 * count)]
where the time goes in v2:
time: 58.9 us; the launch traced here: 58.7 us
  Pallas kernels  58.1 us (99%)
  between operations  0.65 us (1%)
    pallas_call x1, Pallas kernels, body(): pl.pallas_call(functools.partial(step_kernel, splits, per, chunk, section...  56.6 us
    pallas_call x1, Pallas kernels, body(): pl.pallas_call(finish_kernel, out_shape=(jax.ShapeDtypeStruct(latent.shap...  1.45 us

profile of v2, /device:TPU:0, one launch (start us, length us, event | category | flops | bytes accessed | tf_op | source)
XLA Modules:
  0.0 58.7 jit_solution(2365196398039495983)
XLA Ops:
  0.6 56.6 %shard_map.185 = (f32[64,64]{1,0:T(8,128)}, f32[2,3,4,512]{3,2,1,0:T(4,128)}) custom-call(s32[4]{0:T(128)} %amap.1, s32[8]{0:T(128)} %starts.1, f32[64,64]{1,0:T(8,128)} %bitcast.35, bf16[3,64,4096]{2,1,0:T(8,128)(2,1)} %bitcast.26, bf16[3,64,4096]{2,1,0:T(8,128)(2,1)} %bitcast.27, bf16[32,4096]{1,0:T(8,128)(2,1)} %bitcast.32, bf16[64,4096]{1,0:T(8,128)(2,1)} %bitcast.30, ...), custom_call_target="tpu_custom_call" | custom-call | tf_op jit(solution)/shard_map/pallas_call | solution.py:783
  57.2 1.5 %shard_map.186 = (f32[64,64]{1,0:T(8,128)}, f32[3,8,512]{2,1,0:T(8,128)}) custom-call(f32[64,64]{1,0:T(8,128)} %get-tuple-element.6.handed, f32[2,3,4,512]{3,2,1,0:T(4,128)} %get-tuple-element.7.image), custom_call_target="tpu_custom_call" | custom-call | tf_op jit(solution)/shard_map/pallas_call | solution.py:821

commit v3 on v2

--- a/solution.py
+++ b/solution.py
@@ -611,12 +611,6 @@
             put(x2, 2 * t + j,
                 base.astype(F32) + y[4 * j * cols : 4 * (j + 1) * cols].reshape(base.shape))
 
-    @pl.when(jnp.logical_not(last))
-    def _():
-        for c in range(chunks):
-            attend(c)
-        send_parts()
-
     for a in range(2):
         taps = []
         for p in (0, 1):
@@ -641,8 +635,9 @@
 
     @pl.when(jnp.logical_not(last))
     def _():
-        settle()
-        given.start()
+        for c in range(chunks):
+            attend(c)
+        send_parts()
 
     for t in range(3):
         taps = []
@@ -709,6 +704,11 @@
     )
     shared.start()
     shown.start()
+
+    @pl.when(jnp.logical_not(last))
+    def _():
+        settle()
+        given.start()
 
     given.wait_recv()
     given.wait_send()

time: 58.9 us -> 57 us (0.968)
  Pallas kernels: 58.1 us -> 56.2 us
    pallas_call x1, Pallas kernels: 56.6 us -> 54.8 us  [body(): pl.pallas_call(functools.partial(step_kernel, splits, per, chunk, section...]
where the time goes in v3:
time: 57 us; the launch traced here: 56.9 us
  Pallas kernels  56.2 us (99%)
  between operations  0.65 us (1%)
    pallas_call x1, Pallas kernels, body(): pl.pallas_call(functools.partial(step_kernel, splits, per, chunk, section...  54.8 us
    pallas_call x1, Pallas kernels, body(): pl.pallas_call(finish_kernel, out_shape=(jax.ShapeDtypeStruct(latent.shap...  1.45 us

profile of v3, /device:TPU:0, one launch (start us, length us, event | category | flops | bytes accessed | tf_op | source)
XLA Modules:
  0.0 56.9 jit_solution(5280867580187884713)
XLA Ops:
  0.6 54.8 %shard_map.185 = (f32[64,64]{1,0:T(8,128)}, f32[2,3,4,512]{3,2,1,0:T(4,128)}) custom-call(s32[4]{0:T(128)} %amap.1, s32[8]{0:T(128)} %starts.1, f32[64,64]{1,0:T(8,128)} %bitcast.35, bf16[3,64,4096]{2,1,0:T(8,128)(2,1)} %bitcast.26, bf16[3,64,4096]{2,1,0:T(8,128)(2,1)} %bitcast.27, bf16[32,4096]{1,0:T(8,128)(2,1)} %bitcast.32, bf16[64,4096]{1,0:T(8,128)(2,1)} %bitcast.30, ...), custom_call_target="tpu_custom_call" | custom-call | tf_op jit(solution)/shard_map/pallas_call | solution.py:783
  55.4 1.5 %shard_map.186 = (f32[64,64]{1,0:T(8,128)}, f32[3,8,512]{2,1,0:T(8,128)}) custom-call(f32[64,64]{1,0:T(8,128)} %get-tuple-element.6.handed, f32[2,3,4,512]{3,2,1,0:T(4,128)} %get-tuple-element.7.image), custom_call_target="tpu_custom_call" | custom-call | tf_op jit(solution)/shard_map/pallas_call | solution.py:821

commit v4 on v3

--- a/solution.py
+++ b/solution.py
@@ -635,9 +635,8 @@
 
     @pl.when(jnp.logical_not(last))
     def _():
-        for c in range(chunks):
+        for c in range(chunks - 1):
             attend(c)
-        send_parts()
 
     for t in range(3):
         taps = []
@@ -661,6 +660,11 @@
             ])
             value = (a3[2 * t + 1 + j].astype(F32) + value).astype(BF16).astype(F32)
             put(p4, 2 * t + j, act(value, g4))
+
+    @pl.when(jnp.logical_not(last))
+    def _():
+        attend(chunks - 1)
+        send_parts()
 
     p4[0] = scaled(p4[0], keep[21])
     p4[5] = scaled(p4[5], keep[23])

time: 57 us -> 58.9 us (1.033)
  Pallas kernels: 56.2 us -> 58 us
    pallas_call x1, Pallas kernels: 54.8 us -> 56.6 us  [body(): pl.pallas_call(functools.partial(step_kernel, splits, per, chunk, section...]
where the time goes in v4:
time: 58.9 us; the launch traced here: 58.7 us
  Pallas kernels  58 us (98%)
  between operations  0.65 us (1%)
    pallas_call x1, Pallas kernels, body(): pl.pallas_call(functools.partial(step_kernel, splits, per, chunk, section...  56.6 us
    pallas_call x1, Pallas kernels, body(): pl.pallas_call(finish_kernel, out_shape=(jax.ShapeDtypeStruct(latent.shap...  1.45 us

profile of v4, /device:TPU:0, one launch (start us, length us, event | category | flops | bytes accessed | tf_op | source)
XLA Modules:
  0.0 58.7 jit_solution(3760458897253342243)
XLA Ops:
  0.6 56.6 %shard_map.185 = (f32[64,64]{1,0:T(8,128)}, f32[2,3,4,512]{3,2,1,0:T(4,128)}) custom-call(s32[4]{0:T(128)} %amap.1, s32[8]{0:T(128)} %starts.1, f32[64,64]{1,0:T(8,128)} %bitcast.35, bf16[3,64,4096]{2,1,0:T(8,128)(2,1)} %bitcast.26, bf16[3,64,4096]{2,1,0:T(8,128)(2,1)} %bitcast.27, bf16[32,4096]{1,0:T(8,128)(2,1)} %bitcast.32, bf16[64,4096]{1,0:T(8,128)(2,1)} %bitcast.30, ...), custom_call_target="tpu_custom_call" | custom-call | tf_op jit(solution)/shard_map/pallas_call | solution.py:787
  57.2 1.5 %shard_map.186 = (f32[64,64]{1,0:T(8,128)}, f32[3,8,512]{2,1,0:T(8,128)}) custom-call(f32[64,64]{1,0:T(8,128)} %get-tuple-element.6.handed, f32[2,3,4,512]{3,2,1,0:T(4,128)} %get-tuple-element.7.image), custom_call_target="tpu_custom_call" | custom-call | tf_op jit(solution)/shard_map/pallas_call | solution.py:825
